TPU v7x, 32 devices: a whole 2x2x4 slice. The times are simulated.
32 devices in a mesh: kcol: 8 (over y, x, core), ion: 4 (over z).
Axes of the slice: x: 2, y: 2, z: 4, core: 2. Of those that a mesh axis runs over, the one named last changes fastest.
Arguments:
- ions: float32 [4, 81920], P(None, ('kcol', 'ion')), may hold values from -1.5 to 1.5, as said below
- col_ids: int32 [1024], P('kcol'), may hold values from 0 to 4095, as said below
Outputs:
- ion_forces: float32 [4, 81920], P(None, ('kcol', 'ion'))
- energy: float32 [], replicated
Inputs may be any that keep to these rules, and one draw needn't show every extreme that they name: `col_ids`: distinct column numbers. `ions`: rows 0 to 2 lie in [0, 1); row 3 has magnitudes 0.5 to 1.5.
All inputs are finite; a program needn't handle non-finite values.
Results may differ from a plain program's by a relative error of at most 0.0003.
Values sent between devices are 32-bit elements; how exact they have to be, the bound alone decides.
No kernel may reach another device: no remote copies, remote signals or barrier semaphores. Data moves between devices by JAX's collectives and lax.ppermute only.
A program may use at most 64 MiB of HBM per device.

v0:
```python
import math
import jax
import jax.numpy as jnp
from jax import lax
from jax.sharding import PartitionSpec as P

KX = 32


def wave_numbers(col_ids):
    wave_x = jnp.arange(KX, dtype=jnp.int32)
    wave_y = col_ids // 64 - 32
    wave_z = col_ids % 64 - 32
    return (wave_x, wave_y, wave_z)


def kspace_weight(wave_x, wave_y, wave_z):
    radial = wave_y * wave_y + wave_z * wave_z
    along = wave_x * wave_x
    squared = along[:, None] + radial[None, :]
    inside = (squared <= 1024) & (squared > 0)
    squared_f = squared.astype(jnp.float32)
    halving = jnp.where(wave_x == 0, jnp.float32(0.5), jnp.float32(1.0))[:, None]
    return jnp.where(
        inside,
        halving * jnp.exp(-squared_f / 1600.0) / jnp.maximum(squared_f, 1.0),
        jnp.float32(0.0),
    )


def phase_tables(block, wave_x, wave_y, wave_z):
    two_pi = 2.0 * math.pi
    angle_x = two_pi * wave_x.astype(jnp.float32)[:, None] * block[0][None, :]
    angle_yz = two_pi * (
        wave_y.astype(jnp.float32)[:, None] * block[1][None, :]
        + wave_z.astype(jnp.float32)[:, None] * block[2][None, :]
    )
    return (jnp.cos(angle_x), jnp.sin(angle_x), jnp.cos(angle_yz), jnp.sin(angle_yz))


def factor_piece(block, waves):
    cos_x, sin_x, cos_yz, sin_yz = phase_tables(block, *waves)
    charge = block[3][None, :]
    left = jnp.concatenate([charge * cos_x, charge * sin_x], 0)
    right = jnp.concatenate([cos_yz, sin_yz], 0)
    product = lax.dot_general(
        left,
        right,
        (((1,), (1,)), ((), ())),
        precision=lax.Precision.HIGHEST,
        preferred_element_type=jnp.float32,
    )
    nwave = cos_x.shape[0]
    ncol = cos_yz.shape[0]
    real_part = product[:nwave, :ncol] - product[nwave:, ncol:]
    imag_part = product[:nwave, ncol:] + product[nwave:, :ncol]
    return jnp.stack([real_part, imag_part])


def combine_matrix(weight, factor, wave_x):
    g_real = weight * factor[0]
    g_imag = -weight * factor[1]
    scaled = wave_x.astype(jnp.float32)[:, None]
    x_real = scaled * g_real
    x_imag = scaled * g_imag
    return jnp.concatenate(
        [
            jnp.concatenate([g_real.T, -g_imag.T], 1),
            jnp.concatenate([g_imag.T, g_real.T], 1),
            jnp.concatenate([x_real.T, -x_imag.T], 1),
            jnp.concatenate([x_imag.T, x_real.T], 1),
        ],
        0,
    )


def force_piece(block, combined, waves, force_scale, potential_scale):
    cos_x, sin_x, cos_yz, sin_yz = phase_tables(block, *waves)
    basis = jnp.concatenate([cos_x, sin_x], 0)
    spread = jnp.dot(
        combined, basis, precision=lax.Precision.HIGHEST, preferred_element_type=jnp.float32
    )
    ncol = cos_yz.shape[0]
    h_real0 = spread[:ncol]
    h_imag0 = spread[ncol : 2 * ncol]
    h_real1 = spread[2 * ncol : 3 * ncol]
    h_imag1 = spread[3 * ncol :]
    imag_zero = h_real0 * sin_yz + h_imag0 * cos_yz
    real_zero = h_real0 * cos_yz - h_imag0 * sin_yz
    imag_one = h_real1 * sin_yz + h_imag1 * cos_yz
    charge = block[3]
    wave_y = waves[1].astype(jnp.float32)[:, None]
    wave_z = waves[2].astype(jnp.float32)[:, None]
    force_x = force_scale * charge * jnp.sum(imag_one, 0)
    force_y = force_scale * charge * jnp.sum(wave_y * imag_zero, 0)
    force_z = force_scale * charge * jnp.sum(wave_z * imag_zero, 0)
    potential = potential_scale * jnp.sum(real_zero, 0)
    return jnp.stack([force_x, force_y, force_z, potential])


def per_device(ions, col_ids):
    groups = lax.axis_size("kcol")
    piece = ions.shape[1]
    total = piece * groups * lax.axis_size("ion")
    waves = wave_numbers(col_ids)
    weight = kspace_weight(*waves)
    ncol = col_ids.shape[0]
    gathered = lax.all_gather(ions, "kcol", axis=1, tiled=True)

    def add_factor(piece_index, partial_value):
        block = lax.dynamic_slice_in_dim(gathered, piece_index * piece, piece, 1)
        return partial_value + factor_piece(block, waves)

    partial_value = lax.fori_loop(0, groups, add_factor, jnp.zeros((2, KX, ncol), jnp.float32))
    factor = lax.psum(partial_value, "ion")
    energy_group = jnp.float32(0.01 / total) * jnp.sum(
        weight * (factor[0] * factor[0] + factor[1] * factor[1])
    )
    combined = combine_matrix(weight, factor, waves[0])
    force_scale = jnp.float32(0.04 * math.pi / math.sqrt(total))
    potential_scale = jnp.float32(0.4 / math.sqrt(total))

    def place_forces(piece_index, result):
        block = lax.dynamic_slice_in_dim(gathered, piece_index * piece, piece, 1)
        return lax.dynamic_update_slice_in_dim(
            result,
            force_piece(block, combined, waves, force_scale, potential_scale),
            piece_index * piece,
            1,
        )

    row_forces = lax.fori_loop(0, groups, place_forces, jnp.zeros((4, groups * piece), jnp.float32))
    summed, energy = lax.psum((row_forces, energy_group), "kcol")
    owned = lax.dynamic_slice_in_dim(summed, lax.axis_index("kcol") * piece, piece, 1)
    return (owned, energy)


def solution(mesh):
    return jax.shard_map(
        per_device,
        mesh=mesh,
        in_specs=(P(None, ("kcol", "ion")), P("kcol")),
        out_specs=(P(None, ("kcol", "ion")), P()),
        check_vma=False,
    )
```

profile of v0, /device:TPU:0, one launch (start us, length us, event | category | flops | bytes accessed | tf_op | source)
XLA Modules:
  0.0 265.6 jit_solution(9668760638139759695)
XLA Ops:
  7.9 11.2 %all_gather.3 = f32[4,20480]{1,0:T(4,128)S(1)} all-gather(f32[4,2560]{1,0:T(4,128)} %param.6), channel_id=1, replica_groups=mesh['kcol'=8,'ion'=4] {'kcol'}, dimensions={1}, use_global_device_ids=true | all-gather | bytes 368640 | tf_op jit(solution)/shard_map/all_gather | solution.py:108
  19.1 70.5 %while.33 = (s32[]{:T(128)}, f32[2,32,128]{2,1,0:T(8,128)S(1)}, f32[4,20480]{1,0:T(4,128)S(1)}, f32[128,1]{0,1:T(1,128)S(1)}, f32[128,1]{0,1:T(1,128)S(1)}, /*in...) while((s32[]{:T(128)}, f32[2,32,128]{2,1,0:T(8,128)S(1)}, ...), condition=%wide.region_1.2_spmd.clone, body=%wide.region_0.1_spmd.clone.sunk | while | flops 505724992 | bytes 6940129 | solution.py:114
  19.2 4.8 %fusion.62 = (f32[128,2560]{1,0:T(8,128)S(1)}, f32[128,2560]{1,0:T(8,128)S(1)}) fusion(f32[2560]{0:T(1024)S(1)} %get-tuple-element.535, f32[128]{0:T(128)S(1)} %bitcast.69, f32[2560]{0:T(1024)S(1)} %get-tuple-element.536, f32[128]{0:T(128)S(1)} %bitcast.71), kind=kLoop, calls=%fused_computation.37.clone.1 | loop fusion | flops 1310720 | bytes 2642944 | tf_op jit(solution)/shard_map/while/body/eval_jaxpr/cos | solution.py:38
  28.1 4.8 %fusion.62 = (f32[128,2560]{1,0:T(8,128)S(1)}, f32[128,2560]{1,0:T(8,128)S(1)}) fusion(f32[2560]{0:T(1024)S(1)} %get-tuple-element.535, f32[128]{0:T(128)S(1)} %bitcast.69, f32[2560]{0:T(1024)S(1)} %get-tuple-element.536, f32[128]{0:T(128)S(1)} %bitcast.71), kind=kLoop, calls=%fused_computation.37.clone.1 | loop fusion | flops 1310720 | bytes 2642944 | tf_op jit(solution)/shard_map/while/body/eval_jaxpr/cos | solution.py:38
  36.9 4.8 %fusion.62 = (f32[128,2560]{1,0:T(8,128)S(1)}, f32[128,2560]{1,0:T(8,128)S(1)}) fusion(f32[2560]{0:T(1024)S(1)} %get-tuple-element.535, f32[128]{0:T(128)S(1)} %bitcast.69, f32[2560]{0:T(1024)S(1)} %get-tuple-element.536, f32[128]{0:T(128)S(1)} %bitcast.71), kind=kLoop, calls=%fused_computation.37.clone.1 | loop fusion | flops 1310720 | bytes 2642944 | tf_op jit(solution)/shard_map/while/body/eval_jaxpr/cos | solution.py:38
  45.7 4.8 %fusion.62 = (f32[128,2560]{1,0:T(8,128)S(1)}, f32[128,2560]{1,0:T(8,128)S(1)}) fusion(f32[2560]{0:T(1024)S(1)} %get-tuple-element.535, f32[128]{0:T(128)S(1)} %bitcast.69, f32[2560]{0:T(1024)S(1)} %get-tuple-element.536, f32[128]{0:T(128)S(1)} %bitcast.71), kind=kLoop, calls=%fused_computation.37.clone.1 | loop fusion | flops 1310720 | bytes 2642944 | tf_op jit(solution)/shard_map/while/body/eval_jaxpr/cos | solution.py:38
  54.5 4.8 %fusion.62 = (f32[128,2560]{1,0:T(8,128)S(1)}, f32[128,2560]{1,0:T(8,128)S(1)}) fusion(f32[2560]{0:T(1024)S(1)} %get-tuple-element.535, f32[128]{0:T(128)S(1)} %bitcast.69, f32[2560]{0:T(1024)S(1)} %get-tuple-element.536, f32[128]{0:T(128)S(1)} %bitcast.71), kind=kLoop, calls=%fused_computation.37.clone.1 | loop fusion | flops 1310720 | bytes 2642944 | tf_op jit(solution)/shard_map/while/body/eval_jaxpr/cos | solution.py:38
  63.3 4.8 %fusion.62 = (f32[128,2560]{1,0:T(8,128)S(1)}, f32[128,2560]{1,0:T(8,128)S(1)}) fusion(f32[2560]{0:T(1024)S(1)} %get-tuple-element.535, f32[128]{0:T(128)S(1)} %bitcast.69, f32[2560]{0:T(1024)S(1)} %get-tuple-element.536, f32[128]{0:T(128)S(1)} %bitcast.71), kind=kLoop, calls=%fused_computation.37.clone.1 | loop fusion | flops 1310720 | bytes 2642944 | tf_op jit(solution)/shard_map/while/body/eval_jaxpr/cos | solution.py:38
  72.2 4.8 %fusion.62 = (f32[128,2560]{1,0:T(8,128)S(1)}, f32[128,2560]{1,0:T(8,128)S(1)}) fusion(f32[2560]{0:T(1024)S(1)} %get-tuple-element.535, f32[128]{0:T(128)S(1)} %bitcast.69, f32[2560]{0:T(1024)S(1)} %get-tuple-element.536, f32[128]{0:T(128)S(1)} %bitcast.71), kind=kLoop, calls=%fused_computation.37.clone.1 | loop fusion | flops 1310720 | bytes 2642944 | tf_op jit(solution)/shard_map/while/body/eval_jaxpr/cos | solution.py:38
  81.0 4.8 %fusion.62 = (f32[128,2560]{1,0:T(8,128)S(1)}, f32[128,2560]{1,0:T(8,128)S(1)}) fusion(f32[2560]{0:T(1024)S(1)} %get-tuple-element.535, f32[128]{0:T(128)S(1)} %bitcast.69, f32[2560]{0:T(1024)S(1)} %get-tuple-element.536, f32[128]{0:T(128)S(1)} %bitcast.71), kind=kLoop, calls=%fused_computation.37.clone.1 | loop fusion | flops 1310720 | bytes 2642944 | tf_op jit(solution)/shard_map/while/body/eval_jaxpr/cos | solution.py:38
  89.6 19.3 %psum.21 = f32[2,32,128]{2,1,0:T(8,128)S(1)} all-reduce(f32[2,32,128]{2,1,0:T(8,128)S(1)} %get-tuple-element.329), channel_id=1, replica_groups=mesh['kcol'=8,'ion'=4] {'ion'}, use_global_device_ids=true, to_apply=%region_2.3 | all-reduce | flops 8192 | bytes 65536 | tf_op jit(solution)/shard_map/psum | solution.py:115
  109.9 95.1 %while.32 = (s32[]{:T(128)}, f32[4,20480]{1,0:T(4,128)S(1)}, f32[4,20480]{1,0:T(4,128)S(1)}, f32[512,64]{1,0:T(8,128)S(1)}, f32[128,1]{0,1:T(1,128)S(1)}, /*inde...) while((s32[]{:T(128)}, f32[4,20480]{1,0:T(4,128)S(1)}, ...), condition=%wide.region_8.9_spmd.clone, body=%wide.region_3.8_spmd.clone.sunk | while | flops 1013137984 | bytes 12256743 | solution.py:132
  115.6 6.0 %multiply_reduce_fusion.4 = (f32[2560]{0:T(1024)S(1)}, f32[2560]{0:T(1024)S(1)}, f32[2560]{0:T(1024)S(1)}, f32[2560]{0:T(1024)S(1)}) fusion(f32[128]{0:T(128)S(1)} %bitcast.72, f32[128]{0:T(128)S(1)} %bitcast.70, f32[512,2560]{1,0:T(8,128)S(1)} %convolution_bitcast_fusion.2, f32[2560]{0:T(1024)S(1)} %get-tuple-element.521, f32[2560]{0:T(1024)S(1)} %get-tuple-element.522), kind=kLoop, calls=%fused_computation.9.clone.1 | loop fusion | flops 6215680 | bytes 5305344 | tf_op jit(solution)/shard_map/while/body/eval_jaxpr/reduce_sum | solution.py:95
  123.1 4.3 %convolution_bitcast_fusion.2 = f32[512,2560]{1,0:T(8,128)S(1)} fusion(f32[512,64]{1,0:T(8,128)S(1)} %get-tuple-element.610, f32[32,2560]{1,0:T(8,128)S(1)} %get-tuple-element.519, f32[32,2560]{1,0:T(8,128)S(1)} %get-tuple-element.520), kind=kOutput, calls=%fused_computation.2.clone.1 | convolution fusion | flops 1006796800 | bytes 6029312 | tf_op jit(solution)/shard_map/while/body/eval_jaxpr/dot_general | solution.py:80
  127.5 6.0 %multiply_reduce_fusion.4 = (f32[2560]{0:T(1024)S(1)}, f32[2560]{0:T(1024)S(1)}, f32[2560]{0:T(1024)S(1)}, f32[2560]{0:T(1024)S(1)}) fusion(f32[128]{0:T(128)S(1)} %bitcast.72, f32[128]{0:T(128)S(1)} %bitcast.70, f32[512,2560]{1,0:T(8,128)S(1)} %convolution_bitcast_fusion.2, f32[2560]{0:T(1024)S(1)} %get-tuple-element.521, f32[2560]{0:T(1024)S(1)} %get-tuple-element.522), kind=kLoop, calls=%fused_computation.9.clone.1 | loop fusion | flops 6215680 | bytes 5305344 | tf_op jit(solution)/shard_map/while/body/eval_jaxpr/reduce_sum | solution.py:95
  139.4 6.0 %multiply_reduce_fusion.4 = (f32[2560]{0:T(1024)S(1)}, f32[2560]{0:T(1024)S(1)}, f32[2560]{0:T(1024)S(1)}, f32[2560]{0:T(1024)S(1)}) fusion(f32[128]{0:T(128)S(1)} %bitcast.72, f32[128]{0:T(128)S(1)} %bitcast.70, f32[512,2560]{1,0:T(8,128)S(1)} %convolution_bitcast_fusion.2, f32[2560]{0:T(1024)S(1)} %get-tuple-element.521, f32[2560]{0:T(1024)S(1)} %get-tuple-element.522), kind=kLoop, calls=%fused_computation.9.clone.1 | loop fusion | flops 6215680 | bytes 5305344 | tf_op jit(solution)/shard_map/while/body/eval_jaxpr/reduce_sum | solution.py:95
  151.2 6.0 %multiply_reduce_fusion.4 = (f32[2560]{0:T(1024)S(1)}, f32[2560]{0:T(1024)S(1)}, f32[2560]{0:T(1024)S(1)}, f32[2560]{0:T(1024)S(1)}) fusion(f32[128]{0:T(128)S(1)} %bitcast.72, f32[128]{0:T(128)S(1)} %bitcast.70, f32[512,2560]{1,0:T(8,128)S(1)} %convolution_bitcast_fusion.2, f32[2560]{0:T(1024)S(1)} %get-tuple-element.521, f32[2560]{0:T(1024)S(1)} %get-tuple-element.522), kind=kLoop, calls=%fused_computation.9.clone.1 | loop fusion | flops 6215680 | bytes 5305344 | tf_op jit(solution)/shard_map/while/body/eval_jaxpr/reduce_sum | solution.py:95
  163.1 6.0 %multiply_reduce_fusion.4 = (f32[2560]{0:T(1024)S(1)}, f32[2560]{0:T(1024)S(1)}, f32[2560]{0:T(1024)S(1)}, f32[2560]{0:T(1024)S(1)}) fusion(f32[128]{0:T(128)S(1)} %bitcast.72, f32[128]{0:T(128)S(1)} %bitcast.70, f32[512,2560]{1,0:T(8,128)S(1)} %convolution_bitcast_fusion.2, f32[2560]{0:T(1024)S(1)} %get-tuple-element.521, f32[2560]{0:T(1024)S(1)} %get-tuple-element.522), kind=kLoop, calls=%fused_computation.9.clone.1 | loop fusion | flops 6215680 | bytes 5305344 | tf_op jit(solution)/shard_map/while/body/eval_jaxpr/reduce_sum | solution.py:95
  170.7 4.3 %convolution_bitcast_fusion.2 = f32[512,2560]{1,0:T(8,128)S(1)} fusion(f32[512,64]{1,0:T(8,128)S(1)} %get-tuple-element.610, f32[32,2560]{1,0:T(8,128)S(1)} %get-tuple-element.519, f32[32,2560]{1,0:T(8,128)S(1)} %get-tuple-element.520), kind=kOutput, calls=%fused_computation.2.clone.1 | convolution fusion | flops 1006796800 | bytes 6029312 | tf_op jit(solution)/shard_map/while/body/eval_jaxpr/dot_general | solution.py:80
  175.0 6.0 %multiply_reduce_fusion.4 = (f32[2560]{0:T(1024)S(1)}, f32[2560]{0:T(1024)S(1)}, f32[2560]{0:T(1024)S(1)}, f32[2560]{0:T(1024)S(1)}) fusion(f32[128]{0:T(128)S(1)} %bitcast.72, f32[128]{0:T(128)S(1)} %bitcast.70, f32[512,2560]{1,0:T(8,128)S(1)} %convolution_bitcast_fusion.2, f32[2560]{0:T(1024)S(1)} %get-tuple-element.521, f32[2560]{0:T(1024)S(1)} %get-tuple-element.522), kind=kLoop, calls=%fused_computation.9.clone.1 | loop fusion | flops 6215680 | bytes 5305344 | tf_op jit(solution)/shard_map/while/body/eval_jaxpr/reduce_sum | solution.py:95
  186.9 6.0 %multiply_reduce_fusion.4 = (f32[2560]{0:T(1024)S(1)}, f32[2560]{0:T(1024)S(1)}, f32[2560]{0:T(1024)S(1)}, f32[2560]{0:T(1024)S(1)}) fusion(f32[128]{0:T(128)S(1)} %bitcast.72, f32[128]{0:T(128)S(1)} %bitcast.70, f32[512,2560]{1,0:T(8,128)S(1)} %convolution_bitcast_fusion.2, f32[2560]{0:T(1024)S(1)} %get-tuple-element.521, f32[2560]{0:T(1024)S(1)} %get-tuple-element.522), kind=kLoop, calls=%fused_computation.9.clone.1 | loop fusion | flops 6215680 | bytes 5305344 | tf_op jit(solution)/shard_map/while/body/eval_jaxpr/reduce_sum | solution.py:95
  198.8 6.0 %multiply_reduce_fusion.4 = (f32[2560]{0:T(1024)S(1)}, f32[2560]{0:T(1024)S(1)}, f32[2560]{0:T(1024)S(1)}, f32[2560]{0:T(1024)S(1)}) fusion(f32[128]{0:T(128)S(1)} %bitcast.72, f32[128]{0:T(128)S(1)} %bitcast.70, f32[512,2560]{1,0:T(8,128)S(1)} %convolution_bitcast_fusion.2, f32[2560]{0:T(1024)S(1)} %get-tuple-element.521, f32[2560]{0:T(1024)S(1)} %get-tuple-element.522), kind=kLoop, calls=%fused_computation.9.clone.1 | loop fusion | flops 6215680 | bytes 5305344 | tf_op jit(solution)/shard_map/while/body/eval_jaxpr/reduce_sum | solution.py:95
  206.4 12.4 %psum.23 = f32[]{:T(128)} all-reduce(f32[]{:T(128)S(6)} %mul_shard_map.3), channel_id=1, replica_groups=mesh['kcol'=8,'ion'=4] {'kcol'}, use_global_device_ids=true, to_apply=%region_11.12 | all-reduce | flops 1 | bytes 8 | tf_op jit(solution)/shard_map/psum | solution.py:133
  218.8 38.5 %all-reduce.2.cloned.1.call-done = f32[4,20480]{1,0:T(4,128)} async-done(((f32[4,20480]{1,0:T(4,128)}), f32[4,20480]{1,0:T(4,128)}) %all-reduce.2.cloned.1.call-update) | async-done | bytes 327696 | tf_op jit(solution)/shard_map/psum | solution.py:133
  (125 shorter events, 73.3 us)
Async XLA Ops:
  7.2 250.2 %all-reduce.2.cloned.1.call-start = ((), (), s32[]{:S(2)}) async-start(), calls=%async_computation | async-start | bytes 655360 | tf_op jit(solution)/shard_map/psum | solution.py:133
  205.0 0.7 copy-start
Sparse Core Ops, SparseCore 0:
  205.9 51.3 all-reduce.1
where the time goes:
time: 266 us
  other arithmetic  109 us (41%)
  matrix products  54.6 us (21%)
  blocking collectives  42.8 us (16%)
  waiting for transfers between devices  38.5 us (14%)
  between operations  14.8 us (6%)
  local copies, waits for them, and re-layouts  4.71 us (2%)
    reduce_sum x8, other arithmetic, force_piece(): force_y = force_scale * charge * jnp.sum(wave_y * imag_zero, 0)  47.9 us
    cos x8, other arithmetic, phase_tables(): jnp.cos(angle_yz)  38.6 us
    psum x1, waiting for transfers between devices, per_device(): summed, energy = lax.psum((row_forces, energy_group), 'kcol')  38.5 us
    dot_general x8, matrix products, force_piece(): jnp.dot(combined, basis, precision=lax.Precision.HIGHEST, preferred_eleme...  34.5 us
    dot_general x8, matrix products, factor_piece(): lax.dot_general(left, right, (((1,), (1,)), ((), ())), precision=lax.Prec...  20.1 us
    psum x1, blocking collectives, per_device(): factor = lax.psum(partial_value, 'ion')  19.3 us
    psum x1, blocking collectives, per_device(): summed, energy = lax.psum((row_forces, energy_group), 'kcol')  12.4 us
    all_gather x1, blocking collectives, per_device(): gathered = lax.all_gather(ions, 'kcol', axis=1, tiled=True)  11.2 us
  transfers between devices with their start and end apart: 1, of which 1 were waited for; matrix products, arithmetic and copies ran while one was open for 0% of the time, Pallas kernels for 0%

commit v1 on v0

--- a/solution.py
+++ b/solution.py
@@ -112,7 +112,7 @@
         return partial_value + factor_piece(block, waves)
 
     partial_value = lax.fori_loop(0, groups, add_factor, jnp.zeros((2, KX, ncol), jnp.float32))
-    factor = lax.psum(partial_value, "ion")
+    factor = jnp.sum(lax.all_gather(partial_value, "ion"), axis=0)
     energy_group = jnp.float32(0.01 / total) * jnp.sum(
         weight * (factor[0] * factor[0] + factor[1] * factor[1])
     )

time: 266 us -> 263 us (0.989)
  blocking collectives: 42.8 us -> 37.3 us
  waiting for transfers between devices: 38.5 us -> 41.5 us
    psum x1 -> x0, blocking collectives: 19.3 us -> none  [per_device(): factor = lax.psum(partial_value, 'ion')]
    all_gather x0 -> x1, blocking collectives: none -> 13.8 us  [per_device(): factor = jnp.sum(lax.all_gather(partial_value, 'ion'), axis=0)]
    psum x1, waiting for transfers between devices: 38.5 us -> 41.5 us  [per_device(): summed, energy = lax.psum((row_forces, energy_group), 'kcol')]
where the time goes in v1:
time: 263 us
  other arithmetic  109 us (41%)
  matrix products  54.6 us (21%)
  waiting for transfers between devices  41.5 us (16%)
  blocking collectives  37.3 us (14%)
  between operations  14.7 us (6%)
  local copies, waits for them, and re-layouts  4.71 us (2%)
    reduce_sum x8, other arithmetic, force_piece(): force_y = force_scale * charge * jnp.sum(wave_y * imag_zero, 0)  47.9 us
    psum x1, waiting for transfers between devices, per_device(): summed, energy = lax.psum((row_forces, energy_group), 'kcol')  41.5 us
    cos x8, other arithmetic, phase_tables(): jnp.cos(angle_yz)  38.6 us
    dot_general x8, matrix products, force_piece(): jnp.dot(combined, basis, precision=lax.Precision.HIGHEST, preferred_eleme...  34.5 us
    dot_general x8, matrix products, factor_piece(): lax.dot_general(left, right, (((1,), (1,)), ((), ())), precision=lax.Prec...  20.1 us
    all_gather x1, blocking collectives, per_device(): factor = jnp.sum(lax.all_gather(partial_value, 'ion'), axis=0)  13.8 us
    psum x1, blocking collectives, per_device(): summed, energy = lax.psum((row_forces, energy_group), 'kcol')  12.3 us
    all_gather x1, blocking collectives, per_device(): gathered = lax.all_gather(ions, 'kcol', axis=1, tiled=True)  11.2 us
  transfers between devices with their start and end apart: 1, of which 1 were waited for; matrix products, arithmetic and copies ran while one was open for 0% of the time, Pallas kernels for 0%

profile of v1, /device:TPU:0, one launch (start us, length us, event | category | flops | bytes accessed | tf_op | source)
XLA Modules:
  0.0 263.0 jit_solution(4078933226962645434)
XLA Ops:
  7.9 11.2 %all_gather.9 = f32[4,20480]{1,0:T(4,128)S(1)} all-gather(f32[4,2560]{1,0:T(4,128)} %param.6), channel_id=1, replica_groups=mesh['kcol'=8,'ion'=4] {'kcol'}, dimensions={1}, use_global_device_ids=true | all-gather | bytes 368640 | tf_op jit(solution)/shard_map/all_gather | solution.py:108
  19.1 70.5 %while.33 = (s32[]{:T(128)}, f32[2,32,128]{2,1,0:T(8,128)S(1)}, f32[4,20480]{1,0:T(4,128)S(1)}, f32[128,1]{0,1:T(1,128)S(1)}, f32[128,1]{0,1:T(1,128)S(1)}, /*in...) while((s32[]{:T(128)}, f32[2,32,128]{2,1,0:T(8,128)S(1)}, ...), condition=%wide.region_1.2_spmd.clone, body=%wide.region_0.1_spmd.clone.sunk | while | flops 505724992 | bytes 6940129 | solution.py:114
  19.2 4.8 %fusion.62 = (f32[128,2560]{1,0:T(8,128)S(1)}, f32[128,2560]{1,0:T(8,128)S(1)}) fusion(f32[2560]{0:T(1024)S(1)} %get-tuple-element.535, f32[128]{0:T(128)S(1)} %bitcast.71, f32[2560]{0:T(1024)S(1)} %get-tuple-element.536, f32[128]{0:T(128)S(1)} %bitcast.73), kind=kLoop, calls=%fused_computation.37.clone.1 | loop fusion | flops 1310720 | bytes 2642944 | tf_op jit(solution)/shard_map/while/body/eval_jaxpr/cos | solution.py:38
  28.1 4.8 %fusion.62 = (f32[128,2560]{1,0:T(8,128)S(1)}, f32[128,2560]{1,0:T(8,128)S(1)}) fusion(f32[2560]{0:T(1024)S(1)} %get-tuple-element.535, f32[128]{0:T(128)S(1)} %bitcast.71, f32[2560]{0:T(1024)S(1)} %get-tuple-element.536, f32[128]{0:T(128)S(1)} %bitcast.73), kind=kLoop, calls=%fused_computation.37.clone.1 | loop fusion | flops 1310720 | bytes 2642944 | tf_op jit(solution)/shard_map/while/body/eval_jaxpr/cos | solution.py:38
  36.9 4.8 %fusion.62 = (f32[128,2560]{1,0:T(8,128)S(1)}, f32[128,2560]{1,0:T(8,128)S(1)}) fusion(f32[2560]{0:T(1024)S(1)} %get-tuple-element.535, f32[128]{0:T(128)S(1)} %bitcast.71, f32[2560]{0:T(1024)S(1)} %get-tuple-element.536, f32[128]{0:T(128)S(1)} %bitcast.73), kind=kLoop, calls=%fused_computation.37.clone.1 | loop fusion | flops 1310720 | bytes 2642944 | tf_op jit(solution)/shard_map/while/body/eval_jaxpr/cos | solution.py:38
  45.7 4.8 %fusion.62 = (f32[128,2560]{1,0:T(8,128)S(1)}, f32[128,2560]{1,0:T(8,128)S(1)}) fusion(f32[2560]{0:T(1024)S(1)} %get-tuple-element.535, f32[128]{0:T(128)S(1)} %bitcast.71, f32[2560]{0:T(1024)S(1)} %get-tuple-element.536, f32[128]{0:T(128)S(1)} %bitcast.73), kind=kLoop, calls=%fused_computation.37.clone.1 | loop fusion | flops 1310720 | bytes 2642944 | tf_op jit(solution)/shard_map/while/body/eval_jaxpr/cos | solution.py:38
  54.5 4.8 %fusion.62 = (f32[128,2560]{1,0:T(8,128)S(1)}, f32[128,2560]{1,0:T(8,128)S(1)}) fusion(f32[2560]{0:T(1024)S(1)} %get-tuple-element.535, f32[128]{0:T(128)S(1)} %bitcast.71, f32[2560]{0:T(1024)S(1)} %get-tuple-element.536, f32[128]{0:T(128)S(1)} %bitcast.73), kind=kLoop, calls=%fused_computation.37.clone.1 | loop fusion | flops 1310720 | bytes 2642944 | tf_op jit(solution)/shard_map/while/body/eval_jaxpr/cos | solution.py:38
  63.3 4.8 %fusion.62 = (f32[128,2560]{1,0:T(8,128)S(1)}, f32[128,2560]{1,0:T(8,128)S(1)}) fusion(f32[2560]{0:T(1024)S(1)} %get-tuple-element.535, f32[128]{0:T(128)S(1)} %bitcast.71, f32[2560]{0:T(1024)S(1)} %get-tuple-element.536, f32[128]{0:T(128)S(1)} %bitcast.73), kind=kLoop, calls=%fused_computation.37.clone.1 | loop fusion | flops 1310720 | bytes 2642944 | tf_op jit(solution)/shard_map/while/body/eval_jaxpr/cos | solution.py:38
  72.2 4.8 %fusion.62 = (f32[128,2560]{1,0:T(8,128)S(1)}, f32[128,2560]{1,0:T(8,128)S(1)}) fusion(f32[2560]{0:T(1024)S(1)} %get-tuple-element.535, f32[128]{0:T(128)S(1)} %bitcast.71, f32[2560]{0:T(1024)S(1)} %get-tuple-element.536, f32[128]{0:T(128)S(1)} %bitcast.73), kind=kLoop, calls=%fused_computation.37.clone.1 | loop fusion | flops 1310720 | bytes 2642944 | tf_op jit(solution)/shard_map/while/body/eval_jaxpr/cos | solution.py:38
  81.0 4.8 %fusion.62 = (f32[128,2560]{1,0:T(8,128)S(1)}, f32[128,2560]{1,0:T(8,128)S(1)}) fusion(f32[2560]{0:T(1024)S(1)} %get-tuple-element.535, f32[128]{0:T(128)S(1)} %bitcast.71, f32[2560]{0:T(1024)S(1)} %get-tuple-element.536, f32[128]{0:T(128)S(1)} %bitcast.73), kind=kLoop, calls=%fused_computation.37.clone.1 | loop fusion | flops 1310720 | bytes 2642944 | tf_op jit(solution)/shard_map/while/body/eval_jaxpr/cos | solution.py:38
  89.6 13.8 %all-gather = f32[8,32,128]{2,1,0:T(8,128)S(1)} all-gather(f32[2,32,128]{2,1,0:T(8,128)S(1)} %get-tuple-element.329), channel_id=2, replica_groups=mesh['kcol'=8,'ion'=4] {'ion'}, dimensions={0}, use_global_device_ids=true | all-gather | bytes 163840 | tf_op jit(solution)/shard_map/all_gather | solution.py:115
  104.4 95.1 %while.32 = (s32[]{:T(128)}, f32[4,20480]{1,0:T(4,128)S(1)}, f32[4,20480]{1,0:T(4,128)S(1)}, f32[512,64]{1,0:T(8,128)S(1)}, f32[128,1]{0,1:T(1,128)S(1)}, /*inde...) while((s32[]{:T(128)}, f32[4,20480]{1,0:T(4,128)S(1)}, ...), condition=%wide.region_8.9_spmd.clone, body=%wide.region_3.8_spmd.clone.sunk | while | flops 1013137984 | bytes 12256743 | solution.py:132
  110.1 6.0 %multiply_reduce_fusion.4 = (f32[2560]{0:T(1024)S(1)}, f32[2560]{0:T(1024)S(1)}, f32[2560]{0:T(1024)S(1)}, f32[2560]{0:T(1024)S(1)}) fusion(f32[128]{0:T(128)S(1)} %bitcast.74, f32[128]{0:T(128)S(1)} %bitcast.72, f32[512,2560]{1,0:T(8,128)S(1)} %convolution_bitcast_fusion.2, f32[2560]{0:T(1024)S(1)} %get-tuple-element.521, f32[2560]{0:T(1024)S(1)} %get-tuple-element.522), kind=kLoop, calls=%fused_computation.9.clone.1 | loop fusion | flops 6215680 | bytes 5305344 | tf_op jit(solution)/shard_map/while/body/eval_jaxpr/reduce_sum | solution.py:95
  117.7 4.3 %convolution_bitcast_fusion.2 = f32[512,2560]{1,0:T(8,128)S(1)} fusion(f32[512,64]{1,0:T(8,128)S(1)} %get-tuple-element.610, f32[32,2560]{1,0:T(8,128)S(1)} %get-tuple-element.519, f32[32,2560]{1,0:T(8,128)S(1)} %get-tuple-element.520), kind=kOutput, calls=%fused_computation.2.clone.1 | convolution fusion | flops 1006796800 | bytes 6029312 | tf_op jit(solution)/shard_map/while/body/eval_jaxpr/dot_general | solution.py:80
  122.0 6.0 %multiply_reduce_fusion.4 = (f32[2560]{0:T(1024)S(1)}, f32[2560]{0:T(1024)S(1)}, f32[2560]{0:T(1024)S(1)}, f32[2560]{0:T(1024)S(1)}) fusion(f32[128]{0:T(128)S(1)} %bitcast.74, f32[128]{0:T(128)S(1)} %bitcast.72, f32[512,2560]{1,0:T(8,128)S(1)} %convolution_bitcast_fusion.2, f32[2560]{0:T(1024)S(1)} %get-tuple-element.521, f32[2560]{0:T(1024)S(1)} %get-tuple-element.522), kind=kLoop, calls=%fused_computation.9.clone.1 | loop fusion | flops 6215680 | bytes 5305344 | tf_op jit(solution)/shard_map/while/body/eval_jaxpr/reduce_sum | solution.py:95
  133.9 6.0 %multiply_reduce_fusion.4 = (f32[2560]{0:T(1024)S(1)}, f32[2560]{0:T(1024)S(1)}, f32[2560]{0:T(1024)S(1)}, f32[2560]{0:T(1024)S(1)}) fusion(f32[128]{0:T(128)S(1)} %bitcast.74, f32[128]{0:T(128)S(1)} %bitcast.72, f32[512,2560]{1,0:T(8,128)S(1)} %convolution_bitcast_fusion.2, f32[2560]{0:T(1024)S(1)} %get-tuple-element.521, f32[2560]{0:T(1024)S(1)} %get-tuple-element.522), kind=kLoop, calls=%fused_computation.9.clone.1 | loop fusion | flops 6215680 | bytes 5305344 | tf_op jit(solution)/shard_map/while/body/eval_jaxpr/reduce_sum | solution.py:95
  141.4 4.3 %convolution_bitcast_fusion.2 = f32[512,2560]{1,0:T(8,128)S(1)} fusion(f32[512,64]{1,0:T(8,128)S(1)} %get-tuple-element.610, f32[32,2560]{1,0:T(8,128)S(1)} %get-tuple-element.519, f32[32,2560]{1,0:T(8,128)S(1)} %get-tuple-element.520), kind=kOutput, calls=%fused_computation.2.clone.1 | convolution fusion | flops 1006796800 | bytes 6029312 | tf_op jit(solution)/shard_map/while/body/eval_jaxpr/dot_general | solution.py:80
  145.8 6.0 %multiply_reduce_fusion.4 = (f32[2560]{0:T(1024)S(1)}, f32[2560]{0:T(1024)S(1)}, f32[2560]{0:T(1024)S(1)}, f32[2560]{0:T(1024)S(1)}) fusion(f32[128]{0:T(128)S(1)} %bitcast.74, f32[128]{0:T(128)S(1)} %bitcast.72, f32[512,2560]{1,0:T(8,128)S(1)} %convolution_bitcast_fusion.2, f32[2560]{0:T(1024)S(1)} %get-tuple-element.521, f32[2560]{0:T(1024)S(1)} %get-tuple-element.522), kind=kLoop, calls=%fused_computation.9.clone.1 | loop fusion | flops 6215680 | bytes 5305344 | tf_op jit(solution)/shard_map/while/body/eval_jaxpr/reduce_sum | solution.py:95
  157.7 6.0 %multiply_reduce_fusion.4 = (f32[2560]{0:T(1024)S(1)}, f32[2560]{0:T(1024)S(1)}, f32[2560]{0:T(1024)S(1)}, f32[2560]{0:T(1024)S(1)}) fusion(f32[128]{0:T(128)S(1)} %bitcast.74, f32[128]{0:T(128)S(1)} %bitcast.72, f32[512,2560]{1,0:T(8,128)S(1)} %convolution_bitcast_fusion.2, f32[2560]{0:T(1024)S(1)} %get-tuple-element.521, f32[2560]{0:T(1024)S(1)} %get-tuple-element.522), kind=kLoop, calls=%fused_computation.9.clone.1 | loop fusion | flops 6215680 | bytes 5305344 | tf_op jit(solution)/shard_map/while/body/eval_jaxpr/reduce_sum | solution.py:95
  169.5 6.0 %multiply_reduce_fusion.4 = (f32[2560]{0:T(1024)S(1)}, f32[2560]{0:T(1024)S(1)}, f32[2560]{0:T(1024)S(1)}, f32[2560]{0:T(1024)S(1)}) fusion(f32[128]{0:T(128)S(1)} %bitcast.74, f32[128]{0:T(128)S(1)} %bitcast.72, f32[512,2560]{1,0:T(8,128)S(1)} %convolution_bitcast_fusion.2, f32[2560]{0:T(1024)S(1)} %get-tuple-element.521, f32[2560]{0:T(1024)S(1)} %get-tuple-element.522), kind=kLoop, calls=%fused_computation.9.clone.1 | loop fusion | flops 6215680 | bytes 5305344 | tf_op jit(solution)/shard_map/while/body/eval_jaxpr/reduce_sum | solution.py:95
  181.4 6.0 %multiply_reduce_fusion.4 = (f32[2560]{0:T(1024)S(1)}, f32[2560]{0:T(1024)S(1)}, f32[2560]{0:T(1024)S(1)}, f32[2560]{0:T(1024)S(1)}) fusion(f32[128]{0:T(128)S(1)} %bitcast.74, f32[128]{0:T(128)S(1)} %bitcast.72, f32[512,2560]{1,0:T(8,128)S(1)} %convolution_bitcast_fusion.2, f32[2560]{0:T(1024)S(1)} %get-tuple-element.521, f32[2560]{0:T(1024)S(1)} %get-tuple-element.522), kind=kLoop, calls=%fused_computation.9.clone.1 | loop fusion | flops 6215680 | bytes 5305344 | tf_op jit(solution)/shard_map/while/body/eval_jaxpr/reduce_sum | solution.py:95
  193.3 6.0 %multiply_reduce_fusion.4 = (f32[2560]{0:T(1024)S(1)}, f32[2560]{0:T(1024)S(1)}, f32[2560]{0:T(1024)S(1)}, f32[2560]{0:T(1024)S(1)}) fusion(f32[128]{0:T(128)S(1)} %bitcast.74, f32[128]{0:T(128)S(1)} %bitcast.72, f32[512,2560]{1,0:T(8,128)S(1)} %convolution_bitcast_fusion.2, f32[2560]{0:T(1024)S(1)} %get-tuple-element.521, f32[2560]{0:T(1024)S(1)} %get-tuple-element.522), kind=kLoop, calls=%fused_computation.9.clone.1 | loop fusion | flops 6215680 | bytes 5305344 | tf_op jit(solution)/shard_map/while/body/eval_jaxpr/reduce_sum | solution.py:95
  200.9 12.3 %psum.15 = f32[]{:T(128)} all-reduce(f32[]{:T(128)S(6)} %mul_shard_map.3), channel_id=1, replica_groups=mesh['kcol'=8,'ion'=4] {'kcol'}, use_global_device_ids=true, to_apply=%region_11.12 | all-reduce | flops 1 | bytes 8 | tf_op jit(solution)/shard_map/psum | solution.py:133
  213.3 41.5 %all-reduce.2.cloned.1.call-done = f32[4,20480]{1,0:T(4,128)} async-done(((f32[4,20480]{1,0:T(4,128)}), f32[4,20480]{1,0:T(4,128)}) %all-reduce.2.cloned.1.call-update) | async-done | bytes 327696 | tf_op jit(solution)/shard_map/psum | solution.py:133
  (126 shorter events, 73.3 us)
Async XLA Ops:
  7.2 247.6 %all-reduce.2.cloned.1.call-start = ((), (), s32[]{:S(2)}) async-start(), calls=%async_computation | async-start | bytes 655360 | tf_op jit(solution)/shard_map/psum | solution.py:133
  199.5 0.7 copy-start
Sparse Core Ops, SparseCore 0:
  200.4 54.2 all-reduce.1
